TPU v7x, 128 devices: a whole 4x4x4 slice. The times are simulated.
128 devices in a mesh: row: 8 (over x, z_lo), col: 16 (over z_hi, y, core).
Axes of the slice: x: 4, y: 4, z: 4 (z_hi: 2, z_lo: 2; z = z_hi * 2 + z_lo), core: 2. Of those that a mesh axis runs over, the one named last changes fastest.
Arguments:
- amplitudes: bfloat16 [32, 768, 768], P('row', 'col'), may hold values from -6 to 6
- factors: bfloat16 [64, 768, 768], P('col', 'row'), may hold values from -0.109375 to 0.109375
- counts: int32 [8], replicated, may hold values from 1 to 4, 16 in all
- pair_index: int32 [32, 2], replicated, may hold values from 0 to 23
- occ_energy: float32 [24], replicated, may hold values from -2 to -0.5
- vir_energy: float32 [768], replicated, may hold values from 0.5 to 3
Outputs:
- new_amplitudes: bfloat16 [32, 768, 768], P('row', 'col')
Inputs may be any that keep to these rules, and one draw needn't show every extreme that they name: The counts sum to 2 times the number of owner rows. `pair_index`: entries of slots that are not live are not used.
All inputs are finite; a program needn't handle non-finite values.
Results may differ from a plain program's by a relative error of at most 0.0046.
Values may be sent and summed in bfloat16 or wider, within the bound.
No kernel may reach another device: no remote copies, remote signals or barrier semaphores. Data moves between devices by JAX's collectives and lax.ppermute only.
A program may use at most 64 MiB of HBM per device.

v0:
```python
import jax
import jax.numpy as jnp
from jax import lax
from jax.sharding import PartitionSpec as P

level_shift = 1.0


def per_device(amplitudes, factors, counts, pair_index, occ_energy, vir_energy):
    slot_count = amplitudes.shape[0]
    col_rows = amplitudes.shape[1]
    row_id = lax.axis_index("row")
    col_id = lax.axis_index("col")
    full_factors = lax.all_gather(factors, "row", axis=1, tiled=True)
    local_slots = jnp.arange(slot_count, dtype=jnp.int32)
    own_live = local_slots < counts[row_id]
    held_pairs = lax.dynamic_slice_in_dim(pair_index, row_id * slot_count, slot_count, 0)
    halfway = jnp.einsum(
        "scb,qdb->sqcd",
        lax.all_gather(amplitudes, "col", axis=1, tiled=True),
        full_factors,
        preferred_element_type=jnp.float32,
    ).astype(jnp.bfloat16)
    ladder = lax.psum_scatter(
        jnp.einsum("qac,sqcd->asd", full_factors, halfway, preferred_element_type=jnp.float32),
        "col",
        scatter_dimension=0,
        tiled=True,
    )
    ladder = jnp.transpose(ladder, (1, 0, 2))
    row_energy = lax.dynamic_slice_in_dim(vir_energy, col_id * col_rows, col_rows, 0)
    occupied = jnp.arange(occ_energy.shape[0], dtype=jnp.int32)
    picks = (held_pairs[:, :, None] == occupied[None, None, :]).astype(jnp.float32)
    pair_energy = jnp.sum(picks * occ_energy[None, None, :], axis=(1, 2))
    denominator = row_energy[None, :, None] + vir_energy[None, None, :] - pair_energy[:, None, None]
    amps_float = amplitudes.astype(jnp.float32)
    updated = amps_float - (ladder + denominator * amps_float) / (denominator + level_shift)
    updated = jnp.where(own_live[:, None, None], updated, 0.0).astype(jnp.bfloat16)
    return updated


def solution(mesh):
    in_specs = (P("row", "col", None), P("col", "row", None), P(), P(), P(), P())
    out_specs = P("row", "col", None)
    return jax.shard_map(
        per_device, mesh=mesh, in_specs=in_specs, out_specs=out_specs, check_vma=False
    )
```

profile of v0, /device:TPU:0, one launch (start us, length us, event | category | flops | bytes accessed | tf_op | source)
XLA Modules:
  0.0 402.4 jit_solution(1089132526216509882)
XLA Ops:
  6.5 0.0 copy-start
  6.5 0.0 all-gather.3.cloned.1.call-start
  6.5 0.7 all-gather.3.cloned.1.call-update
  7.3 0.0 all-gather.5.cloned.1.call-start
  7.3 0.7 all-gather.5.cloned.1.call-update
  8.0 0.0 all-reduce.3.cloned.1.call-start
  8.1 103.0 %all-gather.3.cloned.1.call-done = bf16[4,768,768]{2,1,0:T(8,128)(2,1)} async-done(((bf16[4,96,768]{2,1,0:T(8,128)(2,1)}), bf16[4,768,768]{2,1,0:T(8,128)(2,1)}) %all-gather.3.cloned.1.call-update) | async-done | bytes 4718608 | tf_op jit(solution)/shard_map/all_gather | solution.py:14
  111.1 61.7 %all-gather.5.cloned.1.call-done = bf16[4,768,768]{2,1,0:T(8,128)(2,1)} async-done(((bf16[4,48,768]{2,1,0:T(8,128)(2,1)}), bf16[4,768,768]{2,1,0:T(8,128)(2,1)}) %all-gather.5.cloned.1.call-update) | async-done | bytes 4718608 | tf_op jit(solution)/shard_map/all_gather | solution.py:20
  172.7 42.8 %fusion.7 = f32[768,4,768]{0,2,1:T(8,128)} fusion(bf16[4,768,768]{2,1,0:T(8,128)(2,1)} %all-gather.3.cloned.1.call-done, bf16[4,768,768]{2,1,0:T(8,128)(2,1)} %all-gather.5.cloned.1.call-done), kind=kOutput, calls=%fused_computation.7 | convolution fusion | flops 29000466432 | bytes 18874368 | tf_op jit(solution)/shard_map/qac,sqcd->asd/dot_general | solution.py:25
  215.5 12.1 %copy.15 = f32[768,4,768]{2,1,0:T(4,128)} copy(f32[768,4,768]{0,2,1:T(8,128)} %fusion.7) | data formatting | bytes 18874368 | tf_op jit(solution)/shard_map/qac,sqcd->asd/dot_general | solution.py:25
  227.6 0.0 copy-start.5
  227.6 0.0 copy-start.2
  227.6 0.0 copy-start.4
  227.6 0.0 copy-start.3
  227.6 0.0 copy-start.1
  227.6 0.0 all-reduce.3.cloned.1.call-update
  227.7 0.6 copy-done.5
  228.3 0.6 dynamic-slice
  229.5 0.0 copy-done.2
  229.5 0.1 dynamic_slice.10
  229.6 0.0 copy-done.4
  229.6 0.6 dynamic_slice.9
  230.2 0.6 iota_compare_fusion.1
  230.8 0.0 copy-done
  230.8 0.1 constant_dynamic-slice_fusion
  230.9 0.0 copy-done.3
  230.9 0.2 select_reduce_fusion
  231.1 0.1 broadcast_add_fusion
  231.2 162.3 %all-reduce.3.cloned.1.call-done = f32[768,4,768]{2,1,0:T(4,128)} async-done(((f32[768,4,768]{2,1,0:T(4,128)}), f32[768,4,768]{2,1,0:T(4,128)}) %all-reduce.3.cloned.1.call-update) | async-done | bytes 9437200
  393.5 0.0 copy-done.1
  393.5 1.6 fusion.21
  395.1 0.7 copy.16
Async XLA Ops:
  6.5 224.3 %copy-start = (s32[32,2]{0,1:T(2,128)S(1)}, s32[32,2]{0,1:T(2,128)}, u32[]{:S(2)}) copy-start(s32[32,2]{0,1:T(2,128)} %param.9) | copy-start | bytes 772
  6.5 104.5 %all-gather.3.cloned.1.call-start = ((), (), s32[]{:S(2)}) async-start(), calls=%async_computation | async-start | bytes 5308416 | tf_op jit(solution)/shard_map/all_gather | solution.py:14
  7.3 165.5 %all-gather.5.cloned.1.call-start = ((), (), s32[]{:S(2)}) async-start(), calls=%async_computation.1 | async-start | bytes 5013504 | tf_op jit(solution)/shard_map/all_gather | solution.py:20
  8.0 385.5 %all-reduce.3.cloned.1.call-start = ((), (), s32[]{:S(2)}) async-start(), calls=%async_computation.2 | async-start | bytes 18874368
  227.6 0.7 copy-start.5
  227.6 1.9 copy-start.2
  227.6 2.0 copy-start.4
  227.6 3.3 copy-start.3
  227.6 165.9 %copy-start.1 = (bf16[4,48,768]{2,1,0:T(8,128)(2,1)S(1)}, bf16[4,48,768]{2,1,0:T(8,128)(2,1)}, u32[]{:S(2)}) copy-start(bf16[4,48,768]{2,1,0:T(8,128)(2,1)} %param.6) | copy-start | bytes 884740
Sparse Core Ops, SparseCore 0:
  9.0 102.0 all-gather.2
  113.5 59.1 all-gather.4
  227.8 165.7 all-reduce.2
where the time goes:
time: 403 us; the launch traced here: 402 us
  waiting for transfers between devices  328 us (81%)
  matrix products  42.8 us (11%)
  local copies, waits for them, and re-layouts  14.7 us (4%)
  between operations  13.8 us (3%)
    unnamed x4, waiting for transfers between devices  164 us
    all_gather x1, waiting for transfers between devices, per_device(): full_factors = lax.all_gather(factors, 'row', axis=1, tiled=True)  103 us
    all_gather x1, waiting for transfers between devices, per_device(): lax.all_gather(amplitudes, 'col', axis=1, tiled=True)  61.7 us
    dot_general x1, matrix products, per_device(): jnp.einsum('qac,sqcd->asd', full_factors, halfway, preferred_element_type...  42.8 us
    dot_general x1, local copies, waits for them, and re-layouts, per_device(): jnp.einsum('qac,sqcd->asd', full_factors, halfway, preferred_element_type...  12.1 us
  transfers between devices with their start and end apart: 3, of which 3 were waited for; matrix products, arithmetic and copies ran while one was open for 1% of the time, Pallas kernels for 0%

commit v1 on v0

--- a/solution.py
+++ b/solution.py
@@ -11,7 +11,8 @@
     col_rows = amplitudes.shape[1]
     row_id = lax.axis_index("row")
     col_id = lax.axis_index("col")
-    full_factors = lax.all_gather(factors, "row", axis=1, tiled=True)
+    outgoing = jnp.stack([factors] * lax.axis_size("row"))
+    full_factors = jnp.concatenate(lax.all_to_all(outgoing, "row", 0, 0), axis=1)
     local_slots = jnp.arange(slot_count, dtype=jnp.int32)
     own_live = local_slots < counts[row_id]
     held_pairs = lax.dynamic_slice_in_dim(pair_index, row_id * slot_count, slot_count, 0)

time: 403 us -> 326 us (0.81)
  waiting for transfers between devices: 328 us -> 182 us
  blocking collectives: 0 us -> 65.1 us
  local copies, waits for them, and re-layouts: 14.7 us -> 18.8 us
    all_gather x1 -> x0, waiting for transfers between devices: 103 us -> none  [per_device(): full_factors = lax.all_gather(factors, 'row', axis=1, tiled=True)]
    all_to_all x0 -> x1, blocking collectives: none -> 65.1 us  [per_device(): lax.all_to_all(outgoing, 'row', 0, 0)]
    all_gather x1, waiting for transfers between devices: 61.7 us -> 18.6 us  [per_device(): lax.all_gather(amplitudes, 'col', axis=1, tiled=True)]
    unnamed x4 -> x3, waiting for transfers between devices: 164 us -> 163 us
  transfers between devices with their start and end apart: 3 -> 2, of which waited for: 3 -> 2; matrix products, arithmetic and copies ran while one was open for 1% -> 2% of each run, Pallas kernels for 0% -> 0%
where the time goes in v1:
time: 326 us; the launch traced here: 325 us
  waiting for transfers between devices  182 us (56%)
  blocking collectives  65.1 us (20%)
  matrix products  42.8 us (13%)
  local copies, waits for them, and re-layouts  18.8 us (6%)
  between operations  14.1 us (4%)
    unnamed x3, waiting for transfers between devices  163 us
    all_to_all x1, blocking collectives, per_device(): lax.all_to_all(outgoing, 'row', 0, 0)  65.1 us
    dot_general x1, matrix products, per_device(): jnp.einsum('qac,sqcd->asd', full_factors, halfway, preferred_element_type...  42.8 us
    all_gather x1, waiting for transfers between devices, per_device(): lax.all_gather(amplitudes, 'col', axis=1, tiled=True)  18.6 us
    dot_general x1, local copies, waits for them, and re-layouts, per_device(): jnp.einsum('qac,sqcd->asd', full_factors, halfway, preferred_element_type...  12.1 us
  transfers between devices with their start and end apart: 2, of which 2 were waited for; matrix products, arithmetic and copies ran while one was open for 2% of the time, Pallas kernels for 0%

profile of v1, /device:TPU:0, one launch (start us, length us, event | category | flops | bytes accessed | tf_op | source)
XLA Modules:
  0.0 325.3 jit_solution(12509260164452891044)
XLA Ops:
  6.5 0.0 copy-start
  6.5 0.0 all-gather.2.cloned.1.call-start
  6.5 0.7 all-gather.2.cloned.1.call-update
  7.3 0.0 all-reduce.3.cloned.1.call-start
  7.3 1.6 stack.2
  8.9 65.1 %all_to_all.5 = bf16[8,4,96,768]{3,2,1,0:T(8,128)(2,1)S(1)} all-to-all(bf16[8,4,96,768]{3,2,1,0:T(8,128)(2,1)S(1)} %stack.2), channel_id=1, replica_groups=mesh['row'=8,'col'=16] {'row'}, dimensions={0} | all-to-all | bytes 9437184 | tf_op jit(solution)/shard_map/all_to_all | solution.py:15
  74.0 2.5 copy.16
  76.5 18.6 %all-gather.2.cloned.1.call-done = bf16[4,768,768]{2,1,0:T(8,128)(2,1)} async-done(((bf16[4,48,768]{2,1,0:T(8,128)(2,1)}), bf16[4,768,768]{2,1,0:T(8,128)(2,1)}) %all-gather.2.cloned.1.call-update) | async-done | bytes 4718608 | tf_op jit(solution)/shard_map/all_gather | solution.py:21
  95.2 42.8 %fusion.5 = f32[768,4,768]{0,2,1:T(8,128)} fusion(bf16[4,768,768,1]{2,1,0,3:T(8,128)(2,1)} %bitcast.32, bf16[4,768,768]{2,1,0:T(8,128)(2,1)} %all-gather.2.cloned.1.call-done), kind=kOutput, calls=%fused_computation.5 | convolution fusion | flops 29000466432 | bytes 18874368 | tf_op jit(solution)/shard_map/qac,sqcd->asd/dot_general | solution.py:26
  138.0 12.1 %copy.17 = f32[768,4,768]{2,1,0:T(4,128)} copy(f32[768,4,768]{0,2,1:T(8,128)} %fusion.5) | data formatting | bytes 18874368 | tf_op jit(solution)/shard_map/qac,sqcd->asd/dot_general | solution.py:26
  150.1 0.0 copy-start.5
  150.1 0.0 copy-start.2
  150.1 0.0 copy-start.4
  150.1 0.0 copy-start.3
  150.1 0.0 copy-start.1
  150.1 0.0 all-reduce.3.cloned.1.call-update
  150.1 0.6 copy-done.5
  150.7 0.6 dynamic-slice
  152.0 0.0 copy-done.2
  152.0 0.1 dynamic_slice.10
  152.0 0.0 copy-done.4
  152.0 0.6 dynamic_slice.9
  152.6 0.6 iota_compare_fusion.1
  153.3 0.0 copy-done
  153.3 0.1 constant_dynamic-slice_fusion
  153.4 0.0 copy-done.3
  153.4 0.2 select_reduce_fusion
  153.6 0.1 broadcast_add_fusion
  153.6 162.5 %all-reduce.3.cloned.1.call-done = f32[768,4,768]{2,1,0:T(4,128)} async-done(((f32[768,4,768]{2,1,0:T(4,128)}), f32[768,4,768]{2,1,0:T(4,128)}) %all-reduce.3.cloned.1.call-update) | async-done | bytes 9437200
  316.1 0.0 copy-done.1
  316.1 1.6 fusion.13
  317.7 0.7 copy.18
Async XLA Ops:
  6.5 146.8 %copy-start = (s32[32,2]{0,1:T(2,128)S(1)}, s32[32,2]{0,1:T(2,128)}, u32[]{:S(2)}) copy-start(s32[32,2]{0,1:T(2,128)} %param.9) | copy-start | bytes 772
  6.5 88.6 %all-gather.2.cloned.1.call-start = ((), (), s32[]{:S(2)}) async-start(), calls=%async_computation.1 | async-start | bytes 5013504 | tf_op jit(solution)/shard_map/all_gather | solution.py:21
  7.3 308.9 %all-reduce.3.cloned.1.call-start = ((), (), s32[]{:S(2)}) async-start(), calls=%async_computation.2 | async-start | bytes 18874368
  150.1 0.7 copy-start.5
  150.1 1.9 copy-start.2
  150.1 2.0 copy-start.4
  150.1 3.3 %copy-start.3 = (f32[24]{0:T(128)S(1)}, f32[24]{0:T(128)}, u32[]{:S(2)}) copy-start(f32[24]{0:T(128)} %param.10) | copy-start | bytes 292
  150.1 166.1 %copy-start.1 = (bf16[4,48,768]{2,1,0:T(8,128)(2,1)S(1)}, bf16[4,48,768]{2,1,0:T(8,128)(2,1)}, u32[]{:S(2)}) copy-start(bf16[4,48,768]{2,1,0:T(8,128)(2,1)} %param.6) | copy-start | bytes 884740
Sparse Core Ops, SparseCore 0:
  9.8 85.3 all-gather.1
  150.2 165.8 all-reduce.2
